TPU v7x, 32 devices: a whole 2x2x4 slice. The times are simulated.
32 devices in a mesh: groups: 2 (over y), tm: 4 (over z), batch: 2 (over x), rep: 2 (over core).
Axes of the slice: x: 2, y: 2, z: 4, core: 2. Of those that a mesh axis runs over, the one named last changes fastest.
Arguments:
- latents: bfloat16 [8, 2048, 512], P(('groups', 'batch', 'rep'), 'tm'), parts along dimension 0, may hold values from -6 to 6
- session_ids: int32 [8], P(('groups', 'batch', 'rep')), parts along dimension 0, may hold values from 0 to 7
- session_gain: float32 [8, 512], replicated, may hold values from 0.25 to 1.75
- session_shift: float32 [8, 512], replicated, may hold values from -3 to 3
- first_conv_weight: bfloat16 [3, 512, 512], replicated, may hold values from -0.15625 to 0.15625
- first_conv_bias: float32 [512], replicated, may hold values from -1.5 to 1.5
- second_conv_weight: bfloat16 [3, 512, 512], replicated, may hold values from -0.15625 to 0.15625
- second_conv_bias: float32 [512], replicated, may hold values from -1.5 to 1.5
- proj_weight: bfloat16 [512, 128], replicated, may hold values from -0.25 to 0.25
- offsets: int32 [8, 2048], P(('groups', 'batch', 'rep'), 'tm'), parts along dimension 0, may hold values from 1 to 10
- counts: int32 [8, 4], P(('groups', 'batch', 'rep'), 'tm'), parts along dimension 0, may hold values from 128 to 512, as said below
Outputs:
- embedding: bfloat16 [8, 2048, 128], P(('groups', 'batch', 'rep'), 'tm'), parts along dimension 0
- grad_conv: float32 [6, 512, 512], P('groups', None, 'tm'), parts along dimension 0
- grad_bias: float32 [1024], P(('groups', 'tm')), parts along dimension 0
- grad_proj: float32 [1024, 128], P(('groups', 'tm')), parts along dimension 0
There are 2 independent parts, one for each index of `groups`. A program takes and returns all parts, laid end to end along the dimension named above; an argument that names none is the same for every part. Nothing has to cross between parts.
Inputs may be any that keep to these rules, and one draw needn't show every extreme that they name: `counts`: bin t of a slab is live when t is below the slab's count.
All inputs are finite; a program needn't handle non-finite values.
Results may differ from a plain program's by a relative error of at most 0.0063.
Values may be sent and summed in bfloat16 or wider, within the bound.
A program may use at most 64 MiB of HBM per device.

v0:
```python
import jax
import jax.numpy as jnp
from jax import lax
from jax.sharding import PartitionSpec as P

FIRST_DILATION = 1
SECOND_DILATION = 2
OFF_MAX = 10
reciprocal_softness = 2.0


def padded_2(block, sides, width):
    for axis, dim in sides:
        count = lax.axis_size(axis)
        forward = [(i, i + 1) for i in range(count - 1)]
        backward = [(target, source) for source, target in forward]
        low = lax.ppermute(
            lax.slice_in_dim(block, block.shape[dim] - width, None, axis=dim), axis, forward
        )
        high = lax.ppermute(lax.slice_in_dim(block, 0, width, axis=dim), axis, backward)
        block = jnp.concatenate([low, block, high], axis=dim)
    return block


def passed_along(value, axis, steps):
    count = lax.axis_size(axis)
    leading, last = (max(0, -steps), min(count, count - steps))
    return lax.ppermute(value, axis, [(source, source + steps) for source in range(leading, last)])


def convolved_rows(padded, couple_coefficient, bias, dilation, count):
    total = jnp.zeros((count, couple_coefficient.shape[2]), jnp.float32) + bias[None, :]
    for filter_tap_index in range(3):
        shifted = padded[filter_tap_index * dilation : filter_tap_index * dilation + count]
        total = total + jnp.dot(
            shifted, couple_coefficient[filter_tap_index], preferred_element_type=jnp.float32
        )
    return total


def pair_weights(embed, piece_embed, portion_valid, own_first):
    cosine_affinity_matrix = reciprocal_softness * lax.dot_general(
        embed, piece_embed, (((1,), (1,)), ((), ())), preferred_element_type=jnp.float32
    )
    local_embedding = own_first + jnp.arange(embed.shape[0])[:, None]
    remote_embedding = jnp.arange(piece_embed.shape[0])[None, :]
    return (
        jnp.where(
            local_embedding != remote_embedding,
            jnp.exp(cosine_affinity_matrix - reciprocal_softness),
            0.0,
        )
        * portion_valid[None, :]
    )


def per_device(
    latents,
    session_ids,
    session_gain,
    session_shift,
    first_conv_weight,
    first_conv_bias,
    second_conv_weight,
    second_conv_bias,
    proj_weight,
    offsets,
    counts,
):
    count_of_rows = latents.shape[1]
    channels = latents.shape[2]
    slab_index = lax.axis_index("tm")
    slab_count = lax.axis_size("tm")
    picker = (session_ids[:, None] == jnp.arange(session_gain.shape[0])[None, :]).astype(
        jnp.float32
    )
    gain_row = jnp.dot(picker, session_gain, precision=lax.Precision.HIGHEST)
    shift_row = jnp.dot(picker, session_shift, precision=lax.Precision.HIGHEST)
    base_offset = (latents[0].astype(jnp.float32) * gain_row + shift_row).astype(jnp.bfloat16)
    input_padded = padded_2(base_offset, (("tm", 0),), FIRST_DILATION)
    first_preactivation = convolved_rows(
        input_padded, first_conv_weight, first_conv_bias, FIRST_DILATION, count_of_rows
    )
    first_hidden = (base_offset.astype(jnp.float32) + jax.nn.gelu(first_preactivation)).astype(
        jnp.bfloat16
    )
    first_padded = padded_2(first_hidden, (("tm", 0),), SECOND_DILATION)
    second_preactivation = convolved_rows(
        first_padded, second_conv_weight, second_conv_bias, SECOND_DILATION, count_of_rows
    )
    hidden_two = (first_hidden.astype(jnp.float32) + jax.nn.gelu(second_preactivation)).astype(
        jnp.bfloat16
    )
    feats = jnp.dot(hidden_two, proj_weight, preferred_element_type=jnp.float32)
    scale = lax.rsqrt(jnp.sum(feats * feats, axis=1) + 1e-06)
    unit = feats * scale[:, None]
    embed = unit.astype(jnp.bfloat16)
    usable_mask_vector = (jnp.arange(count_of_rows) < counts[0, 0]).astype(jnp.float32)
    live_flags = usable_mask_vector.astype(jnp.bfloat16)
    earlier = passed_along(embed[count_of_rows - OFF_MAX :], "tm", 1)
    extended = jnp.concatenate([earlier, embed], axis=0)
    slab_first = slab_index * count_of_rows
    moment = slab_first + jnp.arange(count_of_rows)
    back_time = moment - offsets[0]
    target = jnp.where(back_time >= 0, back_time, moment + offsets[0])
    local_index = target - slab_first + OFF_MAX
    matched_sample_vector = extended[local_index].astype(jnp.float32)
    own_first = lax.axis_index("batch") * count_of_rows
    piece_embed = lax.all_gather(embed, "batch", axis=0, tiled=True)
    portion_valid = lax.all_gather(live_flags, "batch", axis=0, tiled=True)
    couple_coefficient = pair_weights(
        embed, piece_embed, portion_valid.astype(jnp.float32), own_first
    )
    denom = jnp.sum(couple_coefficient, axis=1)
    piece_embed = lax.all_gather(embed.astype(jnp.float32), "batch", axis=0, tiled=True)
    portion_valid = lax.all_gather(usable_mask_vector, "batch", axis=0, tiled=True)
    piece_denom = lax.all_gather(denom, "batch", axis=0, tiled=True)
    add_piece_embed = piece_embed.astype(jnp.bfloat16)
    couple_coefficient = pair_weights(embed, add_piece_embed, portion_valid, own_first)
    soft = (couple_coefficient / denom[:, None]).astype(jnp.bfloat16)
    reverse = (couple_coefficient * usable_mask_vector[:, None] / piece_denom[None, :]).astype(
        jnp.bfloat16
    )
    anchor_sum = jnp.dot(soft, add_piece_embed, preferred_element_type=jnp.float32)
    pooled_sum = jnp.dot(reverse, add_piece_embed, preferred_element_type=jnp.float32)
    anchor_sum, pooled_sum = (anchor_sum, pooled_sum)
    propagated_samples = (
        jnp.zeros((OFF_MAX + count_of_rows, embed.shape[1]), jnp.float32)
        .at[local_index]
        .add(usable_mask_vector[:, None] * embed.astype(jnp.float32))
    )
    returned = passed_along(propagated_samples[:OFF_MAX], "tm", -1)
    pushed_own = propagated_samples[OFF_MAX:].at[count_of_rows - OFF_MAX :].add(returned)
    unit_length_derivative = reciprocal_softness * (
        usable_mask_vector[:, None] * (anchor_sum - matched_sample_vector) + pooled_sum - pushed_own
    )
    along = jnp.sum(unit * unit_length_derivative, axis=1, keepdims=True)
    grad_feat = ((unit_length_derivative - unit * along) * scale[:, None]).astype(jnp.bfloat16)
    grad_proj = lax.dot_general(
        hidden_two, grad_feat, (((0,), (0,)), ((), ())), preferred_element_type=jnp.float32
    )
    grad_hidden = lax.dot_general(
        grad_feat, proj_weight, (((1,), (1,)), ((), ())), preferred_element_type=jnp.float32
    )
    unused, pull = jax.vjp(jax.nn.gelu, second_preactivation)
    gradient_preactivation = pull(grad_hidden)[0].astype(jnp.bfloat16)
    grad_bias = jnp.sum(gradient_preactivation.astype(jnp.float32), axis=0)
    grad_conv = jnp.stack(
        [
            lax.dot_general(
                first_padded[
                    filter_tap_index * SECOND_DILATION : filter_tap_index * SECOND_DILATION
                    + count_of_rows
                ],
                gradient_preactivation,
                (((0,), (0,)), ((), ())),
                preferred_element_type=jnp.float32,
            )
            for filter_tap_index in range(3)
        ]
    )
    share = channels // slab_count
    conv_total, bias_total, proj_total = lax.psum(
        (grad_conv, grad_bias, grad_proj), ("tm", "batch", "rep")
    )
    conv_part = lax.dynamic_slice_in_dim(conv_total, slab_index * share, share, 2)
    bias_part = lax.dynamic_slice_in_dim(bias_total, slab_index * share, share, 0)
    proj_part = lax.dynamic_slice_in_dim(proj_total, slab_index * share, share, 0)
    return (embed[None], conv_part, bias_part, proj_part)


def solution(mesh):
    return jax.shard_map(
        per_device,
        mesh=mesh,
        in_specs=(
            P(("groups", "batch", "rep"), "tm", None),
            P(("groups", "batch", "rep")),
            P(),
            P(),
            P(),
            P(),
            P(),
            P(),
            P(),
            P(("groups", "batch", "rep"), "tm"),
            P(("groups", "batch", "rep"), "tm"),
        ),
        out_specs=(
            P(("groups", "batch", "rep"), "tm", None),
            P("groups", None, "tm"),
            P(("groups", "tm")),
            P(("groups", "tm"), None),
        ),
        check_vma=False,
    )
```

profile of v0, /device:TPU:0, one launch (start us, length us, event | category | flops | bytes accessed | tf_op | source)
XLA Modules:
  0.0 196.3 jit_solution(15781710611473754294)
XLA Ops:
  7.2 0.0 copy-start
  7.2 0.0 copy-start.2
  7.2 0.0 copy-start.3
  7.2 0.0 all-reduce.3.cloned.1.call-start
  8.0 0.8 fusion.55
  8.9 0.8 fusion.53
  9.7 1.2 fusion.6
  10.9 1.3 collective-permute-start.1
  12.2 5.6 %collective-permute-start = (bf16[1,512]{1,0:T(2,128)(2,1)S(1)}, bf16[1,512]{1,0:T(2,128)(2,1)S(1)}, u32[]{:S(2)}, u32[]{:S(2)}) collective-permute-start(bf16[1,512]{1,0:T(2,128)(2,1)S(1)} %get-tuple-element.21), channel_id=1, source_target_pairs={{0,4},{4,8},{8,12},{1,5},{5,9},{9,13},{2,6},{6,10},{10,14},{3,7},{... | collective-permute-start | bytes 3080 | tf_op jit(solution)/shard_map/ppermute | solution.py:17
  18.5 4.3 %all-gather.1 = bf16[2,1,512]{2,1,0:T(2,128)(2,1)S(1)} all-gather(bf16[1,1,512]{2,1,0:T(2,128)(2,1)S(1)} %reshape.147), channel_id=1, replica_groups=mesh['groups'=2,'tm'=4,'batch'=2,'rep'=2] {'batch'}, dimensions={0}, use_global_device_ids=true | all-gather | bytes 3072 | tf_op jit(solution)/shard_map/all_gather | solution.py:110
  22.8 0.7 compare_select_fusion
  23.5 1.6 fusion.27
  25.2 4.3 %all-gather = f32[2,1,512]{2,1,0:T(1,128)S(1)} all-gather(f32[1,1,512]{2,1,0:T(1,128)S(1)} %bitcast.87), channel_id=1, replica_groups=mesh['groups'=2,'tm'=4,'batch'=2,'rep'=2] {'batch'}, dimensions={0}, use_global_device_ids=true | all-gather | bytes 6144 | tf_op jit(solution)/shard_map/all_gather | solution.py:116
  29.5 0.0 collective-permute-done
  29.5 0.0 copy-done.2
  29.5 0.0 copy-done.3
  29.5 0.5 fusion.1
  30.0 0.0 copy-start.1
  30.0 0.0 collective-permute-done.1
  30.0 0.8 fusion.24
  30.8 0.0 copy-start.4
  30.8 1.3 collective-permute-start.3
  32.1 4.5 %collective-permute-start.2 = (bf16[2,512]{1,0:T(2,128)(2,1)S(1)}, bf16[2,512]{1,0:T(2,128)(2,1)S(1)}, u32[]{:S(2)}, u32[]{:S(2)}) collective-permute-start(bf16[2,512]{1,0:T(2,128)(2,1)S(1)} %get-tuple-element.19), channel_id=1, source_target_pairs={{0,4},{4,8},{8,12},{1,5},{5,9},{9,13},{2,6},{6,10},{10,14},{3,7},{... | collective-permute-start | bytes 6152 | tf_op jit(solution)/shard_map/ppermute | solution.py:17
  36.6 0.0 copy-done.1
  36.7 0.4 fusion.32
  37.1 0.8 collective-permute-done.2
  37.9 0.0 copy-done.4
  37.9 0.4 fusion
  38.4 0.0 collective-permute-done.3
  38.4 1.7 add_convert_fusion
  40.1 0.0 copy-done
  40.1 0.4 multiply_reduce_fusion.2
  40.5 0.1 multiply_convert_fusion.1
  40.7 6.7 %all_gather.15 = bf16[1024,128]{1,0:T(8,128)(2,1)S(1)} all-gather(bf16[512,128]{1,0:T(8,128)(2,1)S(1)} %multiply_convert_fusion.1), channel_id=1, replica_groups=mesh['groups'=2,'tm'=4,'batch'=2,'rep'=2] {'batch'}, dimensions={0}, use_global_device_ids=true | all-gather | bytes 393216 | tf_op jit(solution)/shard_map/all_gather | solution.py:115
  47.4 5.6 %all_gather.17 = bf16[1024,128]{1,0:T(8,128)(2,1)S(1)} all-gather(bf16[512,128]{1,0:T(8,128)(2,1)S(1)} %multiply_convert_fusion.1), channel_id=1, replica_groups=mesh['groups'=2,'tm'=4,'batch'=2,'rep'=2] {'batch'}, dimensions={0}, use_global_device_ids=true | all-gather | bytes 393216 | tf_op jit(solution)/shard_map/all_gather | solution.py:109
  53.0 3.9 %collective-permute-start.4 = (bf16[10,128]{1,0:T(8,128)(2,1)S(1)}, bf16[10,128]{1,0:T(8,128)(2,1)S(1)}, u32[]{:S(2)}, u32[]{:S(2)}) collective-permute-start(bf16[10,128]{1,0:T(8,128)(2,1)S(1)} %slice.101), channel_id=1, source_target_pairs={{0,4},{4,8},{8,12},{1,5},{5,9},{9,13},{2,6},{6,10},{10,14},{3,7},{... | collective-permute-start | bytes 7688 | tf_op jit(solution)/shard_map/ppermute | solution.py:28
  56.9 2.5 %scatter_custom_fusion = f32[522,128]{1,0:T(8,128)S(1)} fusion(s32[512]{0:T(512)S(1)} %bitcast.93, f32[]{:T(128)} %constant.57.clone.1, f32[512]{0:T(512)S(1)} %fusion.52, f32[512,128]{1,0:T(8,128)S(1)} %get-tuple-element.25, f32[512]{0:T(512)S(1)} %add_rsqrt_fusion), kind=kCustom, calls=%fused_computation.74 | custom fusion | flops 327680 | bytes 533508 | tf_op jit(solution)/shard_map/scatter-add | solution.py:130
  59.4 1.3 collective-permute-start.5
  60.7 0.9 multiply_reduce_fusion
  61.5 0.7 select_multiply_fusion
  62.3 0.0 copy-start.6
  62.3 0.5 fusion.25
  62.8 0.8 copy-done.6
  63.6 4.3 %all-gather.2 = f32[2,1,512]{2,1,0:T(1,128)S(1)} all-gather(f32[1,1,512]{2,1,0:T(1,128)S(1)} %bitcast.97), channel_id=1, replica_groups=mesh['groups'=2,'tm'=4,'batch'=2,'rep'=2] {'batch'}, dimensions={0}, use_global_device_ids=true | all-gather | bytes 6144 | tf_op jit(solution)/shard_map/all_gather | solution.py:117
  68.0 0.0 collective-permute-done.4
  68.0 1.3 gather_fusion
  69.3 0.0 collective-permute-done.5
  69.4 0.2 scatter-add.13
  69.5 0.0 copy-start.5
  69.6 2.3 %multiply_reduce_fusion.1 = (f32[512]{0:T(512)S(1)}, f32[512,128]{1,0:T(8,128)S(1)}) fusion(f32[512,128]{1,0:T(8,128)S(1)} %get-tuple-element.25, f32[512]{0:T(512)S(1)} %add_rsqrt_fusion, f32[512,128]{1,0:T(8,128)S(1)} %scatter-add.13, bf16[1024,128]{1,0:T(8,128)(2,1)S(1)} %all_gather.15, f32[512,1024]{1,0:T(8,128)} %copy-done.6, f32[1024]{0:T(1024)S(1)} %bitcast.95, ...), kind=kOutput, calls=%fused_computation.73 | convolution fusion | flops 136379904 | bytes 3549184 | tf_op jit(solution)/shard_map/dot_general | solution.py:125
  71.8 0.2 multiply_convert_fusion
  72.1 1.0 fusion.75
  73.1 0.9 convert_reduce_fusion
  74.0 0.5 convolution_bitcast_fusion.1
  74.4 0.5 convolution_bitcast_fusion
  74.9 0.5 convolution_bitcast_fusion.2
  75.4 2.0 %pad_maximum_fusion = f32[3,512,512]{2,1,0:T(8,128)} fusion(f32[1,512,512]{2,1,0:T(8,128)S(1)} %convolution_bitcast_fusion, f32[1,512,512]{2,1,0:T(8,128)S(1)} %convolution_bitcast_fusion.1, f32[1,512,512]{2,1,0:T(8,128)S(1)} %convolution_bitcast_fusion.2), kind=kLoop, calls=%fused_computation.2 | loop fusion | flops 1572864 | bytes 6291456 | tf_op jit(solution)/shard_map/stack | solution.py:148
  77.4 0.0 all-reduce.3.cloned.1.call-update
  77.4 0.8 fusion.95
  78.2 31.1 %psum.22 = f32[512]{0:T(512)S(1)} all-reduce(f32[512]{0:T(512)S(1)} %get-tuple-element.28), channel_id=1, replica_groups=mesh['groups'=2,'tm'=4,'batch'=2,'rep'=2] {'tm','batch','rep'}, use_global_device_ids=true, to_apply=%region_6.7 | all-reduce | flops 512 | bytes 4096 | tf_op jit(solution)/shard_map/psum | solution.py:163
  109.3 0.6 dynamic_slice.10
  109.9 76.0 %all-reduce.3.cloned.1.call-done = (f32[3,512,512]{2,1,0:T(8,128)}, f32[512,128]{1,0:T(8,128)}) async-done(((f32[3,512,512]{2,1,0:T(8,128)}, f32[512,128]{1,0:T(8,128)}), (f32[3,512,512]{2,1,0:T(8,128)}, f32[512,128]{1,0:T(8,128)})) %all-reduce.3.cloned.1.call-update) | async-done | bytes 3407888 | tf_op jit(solution)/shard_map/psum | solution.py:163
  185.9 2.1 %constant_dynamic-slice_fusion.1 = f32[3,512,128]{2,1,0:T(8,128)} fusion(f32[3,512,512]{2,1,0:T(8,128)} %get-tuple-element.16, s32[]{:T(128)S(6)} %select_n.38), kind=kLoop, calls=%fused_computation.103 | loop fusion | bytes 1572868 | tf_op jit(solution)/shard_map/dynamic_slice | solution.py:166
  188.0 1.5 constant_dynamic-slice_fusion
  (15 shorter events, 0.1 us)
Async XLA Ops:
  7.2 33.0 %copy-start = (bf16[512,128]{1,0:T(8,128)(2,1)S(1)}, bf16[512,128]{1,0:T(8,128)(2,1)}, u32[]{:S(2)}) copy-start(bf16[512,128]{1,0:T(8,128)(2,1)} %param.21) | copy-start | bytes 393220
  7.2 22.3 %copy-start.2 = (bf16[3,512,512]{2,1,0:T(8,128)(2,1)S(1)}, bf16[3,512,512]{2,1,0:T(8,128)(2,1)}, u32[]{:S(2)}) copy-start(bf16[3,512,512]{2,1,0:T(8,128)(2,1)} %param.17) | copy-start | bytes 4718596
  7.2 22.3 %copy-start.3 = (f32[512]{0:T(512)S(1)}, f32[512]{0:T(512)}, u32[]{:S(2)}) copy-start(f32[512]{0:T(512)} %param.18) | copy-start | bytes 6148
  7.2 178.7 %all-reduce.3.cloned.1.call-start = ((), (), s32[]{:S(2)}) async-start(), calls=%async_computation | async-start | bytes 6815744 | tf_op jit(solution)/shard_map/psum | solution.py:163
  10.9 19.1 %collective-permute-start.1 = (bf16[1,512]{1,0:T(2,128)(2,1)S(1)}, bf16[1,512]{1,0:T(2,128)(2,1)S(1)}, u32[]{:S(2)}, u32[]{:S(2)}) collective-permute-start(bf16[1,512]{1,0:T(2,128)(2,1)S(1)} %get-tuple-element.20), channel_id=1, source_target_pairs={{4,0},{8,4},{12,8},{5,1},{9,5},{13,9},{6,2},{10,6},{14,10},{7,3},{... | collective-permute-start | bytes 3080 | tf_op jit(solution)/shard_map/ppermute | solution.py:20
  12.2 17.3 %collective-permute-start = (bf16[1,512]{1,0:T(2,128)(2,1)S(1)}, bf16[1,512]{1,0:T(2,128)(2,1)S(1)}, u32[]{:S(2)}, u32[]{:S(2)}) collective-permute-start(bf16[1,512]{1,0:T(2,128)(2,1)S(1)} %get-tuple-element.21), channel_id=1, source_target_pairs={{0,4},{4,8},{8,12},{1,5},{5,9},{9,13},{2,6},{6,10},{10,14},{3,7},{... | collective-permute-start | bytes 3080 | tf_op jit(solution)/shard_map/ppermute | solution.py:17
  30.0 6.7 %copy-start.1 = (bf16[3,512,512]{2,1,0:T(8,128)(2,1)S(1)}, bf16[3,512,512]{2,1,0:T(8,128)(2,1)}, u32[]{:S(2)}) copy-start(bf16[3,512,512]{2,1,0:T(8,128)(2,1)} %param.19) | copy-start | bytes 4718596
  30.8 7.2 %copy-start.4 = (f32[512]{0:T(512)S(1)}, f32[512]{0:T(512)}, u32[]{:S(2)}) copy-start(f32[512]{0:T(512)} %param.20) | copy-start | bytes 6148
  30.8 7.6 %collective-permute-start.3 = (bf16[2,512]{1,0:T(2,128)(2,1)S(1)}, bf16[2,512]{1,0:T(2,128)(2,1)S(1)}, u32[]{:S(2)}, u32[]{:S(2)}) collective-permute-start(bf16[2,512]{1,0:T(2,128)(2,1)S(1)} %get-tuple-element.18), channel_id=1, source_target_pairs={{4,0},{8,4},{12,8},{5,1},{9,5},{13,9},{6,2},{10,6},{14,10},{7,3},{... | collective-permute-start | bytes 6152 | tf_op jit(solution)/shard_map/ppermute | solution.py:20
  32.1 5.8 %collective-permute-start.2 = (bf16[2,512]{1,0:T(2,128)(2,1)S(1)}, bf16[2,512]{1,0:T(2,128)(2,1)S(1)}, u32[]{:S(2)}, u32[]{:S(2)}) collective-permute-start(bf16[2,512]{1,0:T(2,128)(2,1)S(1)} %get-tuple-element.19), channel_id=1, source_target_pairs={{0,4},{4,8},{8,12},{1,5},{5,9},{9,13},{2,6},{6,10},{10,14},{3,7},{... | collective-permute-start | bytes 6152 | tf_op jit(solution)/shard_map/ppermute | solution.py:17
  53.0 15.0 %collective-permute-start.4 = (bf16[10,128]{1,0:T(8,128)(2,1)S(1)}, bf16[10,128]{1,0:T(8,128)(2,1)S(1)}, u32[]{:S(2)}, u32[]{:S(2)}) collective-permute-start(bf16[10,128]{1,0:T(8,128)(2,1)S(1)} %slice.101), channel_id=1, source_target_pairs={{0,4},{4,8},{8,12},{1,5},{5,9},{9,13},{2,6},{6,10},{10,14},{3,7},{... | collective-permute-start | bytes 7688 | tf_op jit(solution)/shard_map/ppermute | solution.py:28
  59.4 10.0 %collective-permute-start.5 = (f32[10,128]{1,0:T(8,128)S(1)}, f32[10,128]{1,0:T(8,128)S(1)}, u32[]{:S(2)}, u32[]{:S(2)}) collective-permute-start(f32[10,128]{1,0:T(8,128)S(1)} %slice.104), channel_id=1, source_target_pairs={{4,0},{8,4},{12,8},{5,1},{9,5},{13,9},{6,2},{10,6},{14,10},{7,3},{... | collective-permute-start | bytes 15368 | tf_op jit(solution)/shard_map/ppermute | solution.py:28
  62.3 1.3 copy-start.6
  69.5 3.6 %copy-start.5 = (f32[512,512]{1,0:T(8,128)S(1)}, f32[512,512]{1,0:T(8,128)}, u32[]{:S(2)}) copy-start(f32[512,512]{1,0:T(8,128)} %get-tuple-element.23) | copy-start | bytes 3145732
Sparse Core Ops, SparseCore 0:
  77.5 108.3 all-reduce.2
where the time goes:
time: 197 us; the launch traced here: 196 us
  waiting for transfers between devices  76.9 us (39%)
  blocking collectives  56.4 us (29%)
  starting transfers between devices  17.9 us (9%)
  between operations  15.8 us (8%)
  matrix products  15.2 us (8%)
  other arithmetic  7.54 us (4%)
  local copies, waits for them, and re-layouts  6.55 us (3%)
    psum x1, waiting for transfers between devices, per_device(): lax.psum((grad_conv, grad_bias, grad_proj), ('tm', 'batch', 'rep'))  76 us
    psum x1, blocking collectives, per_device(): lax.psum((grad_conv, grad_bias, grad_proj), ('tm', 'batch', 'rep'))  31.1 us
    ppermute x2, starting transfers between devices, padded_2(): lax.ppermute(lax.slice_in_dim(block, block.shape[dim] - width, None, axis...  10.1 us
    all_gather x1, blocking collectives, per_device(): lax.all_gather(embed.astype(jnp.float32), 'batch', axis=0, tiled=True)  6.66 us
    all_gather x1, blocking collectives, per_device(): piece_embed = lax.all_gather(embed, 'batch', axis=0, tiled=True)  5.63 us
    dot_general x6, matrix products, convolved_rows(): jnp.dot(shifted, couple_coefficient[filter_tap_index], preferred_element_...  5.48 us
    ppermute x2, starting transfers between devices, passed_along(): lax.ppermute(value, axis, [(source, source + steps) for source in range(l...  5.17 us
    all_gather x1, blocking collectives, per_device(): lax.all_gather(usable_mask_vector, 'batch', axis=0, tiled=True)  4.34 us
  transfers between devices with their start and end apart: 7, of which 2 were waited for; matrix products, arithmetic and copies ran while one was open for 6% of the time, Pallas kernels for 0%

commit v1 on v0

--- a/solution.py
+++ b/solution.py
@@ -1,12 +1,23 @@
+import functools
 import jax
 import jax.numpy as jnp
 from jax import lax
 from jax.sharding import PartitionSpec as P
+from jax.lax import psum
 
 FIRST_DILATION = 1
 SECOND_DILATION = 2
 OFF_MAX = 10
 reciprocal_softness = 2.0
+
+
+def list_stops_all(xx, along_axis, device_axis):
+    for tick in (along_axis, device_axis):
+        xx = psum(xx, axis_name=tick)
+    return xx
+
+
+search_the_body = functools.partial(list_stops_all, along_axis=("batch", "rep"), device_axis="tm")
 
 
 def padded_2(block, sides, width):
@@ -160,9 +171,7 @@
         ]
     )
     share = channels // slab_count
-    conv_total, bias_total, proj_total = lax.psum(
-        (grad_conv, grad_bias, grad_proj), ("tm", "batch", "rep")
-    )
+    conv_total, bias_total, proj_total = search_the_body((grad_conv, grad_bias, grad_proj))
     conv_part = lax.dynamic_slice_in_dim(conv_total, slab_index * share, share, 2)
     bias_part = lax.dynamic_slice_in_dim(bias_total, slab_index * share, share, 0)
     proj_part = lax.dynamic_slice_in_dim(proj_total, slab_index * share, share, 0)

time: 197 us -> 297 us (1.51)
  waiting for transfers between devices: 76.9 us -> 189 us
  blocking collectives: 56.4 us -> 43.4 us
    psum x1 -> x2, waiting for transfers between devices: 76 us -> 189 us  [list_stops_all(): xx = psum(xx, axis_name=tick)]
    psum x1 -> x2, blocking collectives: 31.1 us -> 18.1 us  [list_stops_all(): xx = psum(xx, axis_name=tick)]
  transfers between devices with their start and end apart: 7 -> 8, of which waited for: 2 -> 3; matrix products, arithmetic and copies ran while one was open for 6% -> 4% of each run, Pallas kernels for 0% -> 0%
where the time goes in v1:
time: 297 us; the launch traced here: 296 us
  waiting for transfers between devices  189 us (64%)
  blocking collectives  43.4 us (15%)
  starting transfers between devices  17.9 us (6%)
  between operations  15.8 us (5%)
  matrix products  15.2 us (5%)
  other arithmetic  7.55 us (3%)
  local copies, waits for them, and re-layouts  6.55 us (2%)
    psum x2, waiting for transfers between devices, list_stops_all(): xx = psum(xx, axis_name=tick)  189 us
    psum x2, blocking collectives, list_stops_all(): xx = psum(xx, axis_name=tick)  18.1 us
    ppermute x2, starting transfers between devices, padded_2(): lax.ppermute(lax.slice_in_dim(block, block.shape[dim] - width, None, axis...  10.1 us
    all_gather x1, blocking collectives, per_device(): lax.all_gather(embed.astype(jnp.float32), 'batch', axis=0, tiled=True)  6.66 us
  transfers between devices with their start and end apart: 8, of which 3 were waited for; matrix products, arithmetic and copies ran while one was open for 4% of the time, Pallas kernels for 0%

profile of v1, /device:TPU:0, one launch (start us, length us, event | category | flops | bytes accessed | tf_op | source)
XLA Modules:
  0.0 295.9 jit_solution(2540276817413431687)
XLA Ops:
  7.2 0.0 copy-start
  7.2 0.0 copy-start.2
  7.2 0.0 copy-start.3
  7.2 0.0 all-reduce.5.cloned.1.call-start
  8.0 0.8 fusion.55
  8.9 0.8 fusion.53
  9.7 1.2 fusion.6
  10.9 1.3 collective-permute-start.1
  12.2 5.6 %collective-permute-start = (bf16[1,512]{1,0:T(2,128)(2,1)S(1)}, bf16[1,512]{1,0:T(2,128)(2,1)S(1)}, u32[]{:S(2)}, u32[]{:S(2)}) collective-permute-start(bf16[1,512]{1,0:T(2,128)(2,1)S(1)} %get-tuple-element.23), channel_id=1, source_target_pairs={{0,4},{4,8},{8,12},{1,5},{5,9},{9,13},{2,6},{6,10},{10,14},{3,7},{... | collective-permute-start | bytes 3080 | tf_op jit(solution)/shard_map/ppermute | solution.py:28
  18.5 4.3 %all-gather.1 = bf16[2,1,512]{2,1,0:T(2,128)(2,1)S(1)} all-gather(bf16[1,1,512]{2,1,0:T(2,128)(2,1)S(1)} %reshape.147), channel_id=1, replica_groups=mesh['groups'=2,'tm'=4,'batch'=2,'rep'=2] {'batch'}, dimensions={0}, use_global_device_ids=true | all-gather | bytes 3072 | tf_op jit(solution)/shard_map/all_gather | solution.py:121
  22.8 0.7 compare_select_fusion
  23.5 1.6 fusion.27
  25.2 4.3 %all-gather = f32[2,1,512]{2,1,0:T(1,128)S(1)} all-gather(f32[1,1,512]{2,1,0:T(1,128)S(1)} %bitcast.87), channel_id=1, replica_groups=mesh['groups'=2,'tm'=4,'batch'=2,'rep'=2] {'batch'}, dimensions={0}, use_global_device_ids=true | all-gather | bytes 6144 | tf_op jit(solution)/shard_map/all_gather | solution.py:127
  29.5 0.0 collective-permute-done
  29.5 0.5 fusion.1
  30.0 0.0 copy-start.1
  30.0 0.0 collective-permute-done.1
  30.0 0.8 fusion.24
  30.8 0.0 copy-start.4
  30.8 1.3 collective-permute-start.3
  32.1 4.5 %collective-permute-start.2 = (bf16[2,512]{1,0:T(2,128)(2,1)S(1)}, bf16[2,512]{1,0:T(2,128)(2,1)S(1)}, u32[]{:S(2)}, u32[]{:S(2)}) collective-permute-start(bf16[2,512]{1,0:T(2,128)(2,1)S(1)} %get-tuple-element.21), channel_id=1, source_target_pairs={{0,4},{4,8},{8,12},{1,5},{5,9},{9,13},{2,6},{6,10},{10,14},{3,7},{... | collective-permute-start | bytes 6152 | tf_op jit(solution)/shard_map/ppermute | solution.py:28
  36.7 0.4 fusion.32
  37.1 0.8 collective-permute-done.2
  37.9 0.4 fusion
  38.4 0.0 collective-permute-done.3
  38.4 1.7 add_convert_fusion
  40.1 0.4 multiply_reduce_fusion.2
  40.5 0.1 multiply_convert_fusion.1
  40.7 6.7 %all_gather.15 = bf16[1024,128]{1,0:T(8,128)(2,1)S(1)} all-gather(bf16[512,128]{1,0:T(8,128)(2,1)S(1)} %multiply_convert_fusion.1), channel_id=1, replica_groups=mesh['groups'=2,'tm'=4,'batch'=2,'rep'=2] {'batch'}, dimensions={0}, use_global_device_ids=true | all-gather | bytes 393216 | tf_op jit(solution)/shard_map/all_gather | solution.py:126
  47.4 5.6 %all_gather.17 = bf16[1024,128]{1,0:T(8,128)(2,1)S(1)} all-gather(bf16[512,128]{1,0:T(8,128)(2,1)S(1)} %multiply_convert_fusion.1), channel_id=1, replica_groups=mesh['groups'=2,'tm'=4,'batch'=2,'rep'=2] {'batch'}, dimensions={0}, use_global_device_ids=true | all-gather | bytes 393216 | tf_op jit(solution)/shard_map/all_gather | solution.py:120
  53.0 3.9 %collective-permute-start.4 = (bf16[10,128]{1,0:T(8,128)(2,1)S(1)}, bf16[10,128]{1,0:T(8,128)(2,1)S(1)}, u32[]{:S(2)}, u32[]{:S(2)}) collective-permute-start(bf16[10,128]{1,0:T(8,128)(2,1)S(1)} %slice.101), channel_id=1, source_target_pairs={{0,4},{4,8},{8,12},{1,5},{5,9},{9,13},{2,6},{6,10},{10,14},{3,7},{... | collective-permute-start | bytes 7688 | tf_op jit(solution)/shard_map/ppermute | solution.py:39
  56.9 2.5 scatter_custom_fusion
  59.4 1.3 collective-permute-start.5
  60.7 0.9 multiply_reduce_fusion
  61.5 0.7 select_multiply_fusion
  62.3 0.0 copy-start.6
  62.3 0.5 fusion.25
  62.8 0.8 copy-done.6
  63.6 4.3 %all-gather.2 = f32[2,1,512]{2,1,0:T(1,128)S(1)} all-gather(f32[1,1,512]{2,1,0:T(1,128)S(1)} %bitcast.97), channel_id=1, replica_groups=mesh['groups'=2,'tm'=4,'batch'=2,'rep'=2] {'batch'}, dimensions={0}, use_global_device_ids=true | all-gather | bytes 6144 | tf_op jit(solution)/shard_map/all_gather | solution.py:128
  68.0 0.0 collective-permute-done.4
  68.0 1.3 gather_fusion
  69.4 0.0 collective-permute-done.5
  69.4 0.2 scatter-add.13
  69.6 0.0 copy-start.5
  69.6 2.3 multiply_reduce_fusion.1
  71.9 0.2 multiply_convert_fusion
  72.1 1.0 fusion.75
  73.1 0.0 copy-done.5
  73.1 0.9 convert_reduce_fusion
  74.0 0.5 convolution_bitcast_fusion.1
  74.5 0.5 convolution_bitcast_fusion
  74.9 0.5 convolution_bitcast_fusion.2
  75.4 2.0 pad_maximum_fusion
  77.4 0.0 all-reduce.5.cloned.1.call-update
  77.4 0.0 all-reduce.7.cloned.1.call-start
  77.5 75.4 %all-reduce.5.cloned.1.call-done = (f32[3,512,512]{2,1,0:T(8,128)}, f32[512,128]{1,0:T(8,128)}) async-done(((f32[3,512,512]{2,1,0:T(8,128)}, f32[512,128]{1,0:T(8,128)}), (f32[3,512,512]{2,1,0:T(8,128)}, f32[512,128]{1,0:T(8,128)})) %all-reduce.5.cloned.1.call-update) | async-done | bytes 3407888 | tf_op jit(solution)/shard_map/psum | solution.py:16
  152.9 0.0 all-reduce.7.cloned.1.call-update
  152.9 0.8 fusion.95
  153.7 5.8 %psum.44 = f32[512]{0:T(512)S(1)} all-reduce(f32[512]{0:T(512)S(1)} %get-tuple-element.30), channel_id=1, replica_groups=mesh['groups'=2,'tm'=4,'batch'=2,'rep'=2] {'batch','rep'}, use_global_device_ids=true, to_apply=%region_7.8 | all-reduce | flops 512 | bytes 4096 | tf_op jit(solution)/shard_map/psum | solution.py:16
  159.5 12.3 %psum.45 = f32[512]{0:T(512)S(1)} all-reduce(f32[512]{0:T(512)S(1)} %psum.44), channel_id=1, replica_groups=mesh['groups'=2,'tm'=4,'batch'=2,'rep'=2] {'tm'}, use_global_device_ids=true, to_apply=%region_8.9 | all-reduce | flops 512 | bytes 4096 | tf_op jit(solution)/shard_map/psum | solution.py:16
  171.8 0.6 dynamic_slice.10
  172.4 113.2 %all-reduce.7.cloned.1.call-done = (f32[3,512,512]{2,1,0:T(8,128)}, f32[512,128]{1,0:T(8,128)}) async-done(((f32[3,512,512]{2,1,0:T(8,128)}, f32[512,128]{1,0:T(8,128)}), (f32[3,512,512]{2,1,0:T(8,128)}, f32[512,128]{1,0:T(8,128)})) %all-reduce.7.cloned.1.call-update) | async-done | bytes 3407888 | tf_op jit(solution)/shard_map/psum | solution.py:16
  285.5 2.1 constant_dynamic-slice_fusion.1
  287.6 1.5 constant_dynamic-slice_fusion
  (19 shorter events, 0.1 us)
Async XLA Ops:
  7.2 33.0 %copy-start = (bf16[512,128]{1,0:T(8,128)(2,1)S(1)}, bf16[512,128]{1,0:T(8,128)(2,1)}, u32[]{:S(2)}) copy-start(bf16[512,128]{1,0:T(8,128)(2,1)} %param.21) | copy-start | bytes 393220
  7.2 22.3 %copy-start.2 = (bf16[3,512,512]{2,1,0:T(8,128)(2,1)S(1)}, bf16[3,512,512]{2,1,0:T(8,128)(2,1)}, u32[]{:S(2)}) copy-start(bf16[3,512,512]{2,1,0:T(8,128)(2,1)} %param.17) | copy-start | bytes 4718596
  7.2 22.3 %copy-start.3 = (f32[512]{0:T(512)S(1)}, f32[512]{0:T(512)}, u32[]{:S(2)}) copy-start(f32[512]{0:T(512)} %param.18) | copy-start | bytes 6148
  7.2 145.7 %all-reduce.5.cloned.1.call-start = ((), (), s32[]{:S(2)}) async-start(), calls=%async_computation | async-start | bytes 6815744 | tf_op jit(solution)/shard_map/psum | solution.py:16
  10.9 19.1 %collective-permute-start.1 = (bf16[1,512]{1,0:T(2,128)(2,1)S(1)}, bf16[1,512]{1,0:T(2,128)(2,1)S(1)}, u32[]{:S(2)}, u32[]{:S(2)}) collective-permute-start(bf16[1,512]{1,0:T(2,128)(2,1)S(1)} %get-tuple-element.22), channel_id=1, source_target_pairs={{4,0},{8,4},{12,8},{5,1},{9,5},{13,9},{6,2},{10,6},{14,10},{7,3},{... | collective-permute-start | bytes 3080 | tf_op jit(solution)/shard_map/ppermute | solution.py:31
  12.2 17.3 %collective-permute-start = (bf16[1,512]{1,0:T(2,128)(2,1)S(1)}, bf16[1,512]{1,0:T(2,128)(2,1)S(1)}, u32[]{:S(2)}, u32[]{:S(2)}) collective-permute-start(bf16[1,512]{1,0:T(2,128)(2,1)S(1)} %get-tuple-element.23), channel_id=1, source_target_pairs={{0,4},{4,8},{8,12},{1,5},{5,9},{9,13},{2,6},{6,10},{10,14},{3,7},{... | collective-permute-start | bytes 3080 | tf_op jit(solution)/shard_map/ppermute | solution.py:28
  30.0 6.7 %copy-start.1 = (bf16[3,512,512]{2,1,0:T(8,128)(2,1)S(1)}, bf16[3,512,512]{2,1,0:T(8,128)(2,1)}, u32[]{:S(2)}) copy-start(bf16[3,512,512]{2,1,0:T(8,128)(2,1)} %param.19) | copy-start | bytes 4718596
  30.8 7.2 %copy-start.4 = (f32[512]{0:T(512)S(1)}, f32[512]{0:T(512)}, u32[]{:S(2)}) copy-start(f32[512]{0:T(512)} %param.20) | copy-start | bytes 6148
  30.8 7.6 %collective-permute-start.3 = (bf16[2,512]{1,0:T(2,128)(2,1)S(1)}, bf16[2,512]{1,0:T(2,128)(2,1)S(1)}, u32[]{:S(2)}, u32[]{:S(2)}) collective-permute-start(bf16[2,512]{1,0:T(2,128)(2,1)S(1)} %get-tuple-element.20), channel_id=1, source_target_pairs={{4,0},{8,4},{12,8},{5,1},{9,5},{13,9},{6,2},{10,6},{14,10},{7,3},{... | collective-permute-start | bytes 6152 | tf_op jit(solution)/shard_map/ppermute | solution.py:31
  32.1 5.8 %collective-permute-start.2 = (bf16[2,512]{1,0:T(2,128)(2,1)S(1)}, bf16[2,512]{1,0:T(2,128)(2,1)S(1)}, u32[]{:S(2)}, u32[]{:S(2)}) collective-permute-start(bf16[2,512]{1,0:T(2,128)(2,1)S(1)} %get-tuple-element.21), channel_id=1, source_target_pairs={{0,4},{4,8},{8,12},{1,5},{5,9},{9,13},{2,6},{6,10},{10,14},{3,7},{... | collective-permute-start | bytes 6152 | tf_op jit(solution)/shard_map/ppermute | solution.py:28
  53.0 15.0 %collective-permute-start.4 = (bf16[10,128]{1,0:T(8,128)(2,1)S(1)}, bf16[10,128]{1,0:T(8,128)(2,1)S(1)}, u32[]{:S(2)}, u32[]{:S(2)}) collective-permute-start(bf16[10,128]{1,0:T(8,128)(2,1)S(1)} %slice.101), channel_id=1, source_target_pairs={{0,4},{4,8},{8,12},{1,5},{5,9},{9,13},{2,6},{6,10},{10,14},{3,7},{... | collective-permute-start | bytes 7688 | tf_op jit(solution)/shard_map/ppermute | solution.py:39
  59.4 10.0 %collective-permute-start.5 = (f32[10,128]{1,0:T(8,128)S(1)}, f32[10,128]{1,0:T(8,128)S(1)}, u32[]{:S(2)}, u32[]{:S(2)}) collective-permute-start(f32[10,128]{1,0:T(8,128)S(1)} %slice.104), channel_id=1, source_target_pairs={{4,0},{8,4},{12,8},{5,1},{9,5},{13,9},{6,2},{10,6},{14,10},{7,3},{... | collective-permute-start | bytes 15368 | tf_op jit(solution)/shard_map/ppermute | solution.py:39
  62.3 1.3 copy-start.6
  69.6 3.6 %copy-start.5 = (f32[512,512]{1,0:T(8,128)S(1)}, f32[512,512]{1,0:T(8,128)}, u32[]{:S(2)}) copy-start(f32[512,512]{1,0:T(8,128)} %get-tuple-element.25) | copy-start | bytes 3145732
  77.4 208.1 %all-reduce.7.cloned.1.call-start = ((), (), s32[]{:S(2)}) async-start(), calls=%async_computation.1 | async-start | bytes 6815744 | tf_op jit(solution)/shard_map/psum | solution.py:16
Sparse Core Ops, SparseCore 0:
  77.5 75.3 all-reduce.4
  155.3 130.1 all-reduce.6
